TPU v7x, 128 devices: a whole 4x4x4 slice. The times are simulated.
128 devices in a mesh: row: 8 (over x, core), col: 16 (over z, y).
Axes of the slice: x: 4, y: 4, z: 4, core: 2. Of those that a mesh axis runs over, the one named last changes fastest.
Arguments:
- tiles: bfloat16 [8, 16, 384, 128, 128], P('row', 'col'), may hold values from -0.15625 to 0.15625
- tile_row: int32 [8, 16, 384], P('row', 'col'), may hold values from 0 to 511, as said below
- tile_col: int32 [8, 16, 384], P('row', 'col'), may hold values from 0 to 255
- tile_count: int32 [8, 16], P('row', 'col'), may hold values from 96 to 384, as said below
- vectors: bfloat16 [32, 8, 16, 4096], P(None, 'row', 'col'), may hold values from -6 to 6
Outputs:
- image: bfloat16 [32, 524288], P(None, ('row', 'col'))
- back_image: bfloat16 [32, 8, 16, 4096], P(None, 'row', 'col')
Inputs may be any that keep to these rules, and one draw needn't show every extreme that they name: `tile_count`: some device has exactly 384 live slots. `tile_row`: the slots of each device, live or not, name exactly 12 distinct block rows in each aligned run of 32 block rows.
All inputs are finite; a program needn't handle non-finite values.
Results may differ from a plain program's by a relative error of at most 0.0041.
Values may be sent and summed in bfloat16 or wider, within the bound.
No kernel may reach another device: no remote copies, remote signals or barrier semaphores. Data moves between devices by JAX's collectives and lax.ppermute only.
A program may use at most 128 MiB of HBM per device.

v0:
```python
import jax
import jax.numpy as jnp
from jax import lax
from jax.sharding import PartitionSpec as P


def per_device(tiles, tile_row, tile_col, tile_count, vectors):
    vec_cols = vectors.shape[0]
    tile_size = tiles.shape[-1]
    slot_count = tiles.shape[2]
    local_tiles = tiles[0, 0]
    rows_local = tile_row[0, 0]
    cols_local = tile_col[0, 0]
    live_count = tile_count[0, 0]
    live_mask = (jnp.arange(slot_count, dtype=jnp.int32) < live_count).astype(jnp.float32)
    row_devices = lax.axis_size("row")
    col_devices = lax.axis_size("col")
    gathered = lax.all_gather(vectors, "row", axis=1, tiled=True)
    blk_cols = gathered.shape[1] * gathered.shape[3] // tile_size
    blk_rows = blk_cols * col_devices // row_devices
    col_vectors = gathered.reshape(vec_cols, blk_cols, tile_size)

    def slot_group():
        return (local_tiles, rows_local, cols_local, live_mask)

    def forward_terms(totals, start_slot, group_size):
        tile_block, row_index, col_index, slot_mask = slot_group()
        picked = jnp.take(col_vectors, col_index, axis=1)
        product = jnp.einsum("ksj,sij->ksi", picked, tile_block, preferred_element_type=jnp.float32)
        return totals.at[:, row_index].add(product * slot_mask[None, :, None])

    def sweep(term_fn, totals_zero):
        return term_fn(totals_zero, 0, slot_count)

    forward_sum = sweep(forward_terms, jnp.zeros((vec_cols, blk_rows, tile_size), jnp.float32))
    partial_rows = forward_sum.reshape(vec_cols, blk_rows * tile_size)
    share_sum = lax.psum_scatter(partial_rows, "col", scatter_dimension=1, tiled=True)
    image = share_sum.astype(jnp.bfloat16)
    row_image = lax.all_gather(image, "col", axis=1, tiled=True)
    row_blocks = row_image.reshape(vec_cols, blk_rows, tile_size)

    def backward_terms(totals, start_slot, group_size):
        tile_block, row_index, col_index, slot_mask = slot_group()
        picked = jnp.take(row_blocks, row_index, axis=1)
        product = jnp.einsum("ksi,sij->ksj", picked, tile_block, preferred_element_type=jnp.float32)
        return totals.at[:, col_index].add(product * slot_mask[None, :, None])

    backward_sum = sweep(backward_terms, jnp.zeros((vec_cols, blk_cols, tile_size), jnp.float32))
    partial_cols = backward_sum.reshape(vec_cols, row_devices, 1, vectors.shape[3])
    back_sum = lax.psum_scatter(partial_cols, "row", scatter_dimension=1, tiled=True)
    return (image, back_sum.astype(jnp.bfloat16))


def solution(mesh):
    return jax.shard_map(
        per_device,
        mesh=mesh,
        in_specs=(
            P("row", "col", None, None, None),
            P("row", "col", None),
            P("row", "col", None),
            P("row", "col"),
            P(None, "row", "col", None),
        ),
        out_specs=(P(None, ("row", "col")), P(None, "row", "col", None)),
        check_vma=False,
    )
```

profile of v0, /device:TPU:0, one launch (start us, length us, event | category | flops | bytes accessed | tf_op | source)
XLA Modules:
  0.0 400.8 jit_solution(5015955300966419793)
XLA Ops:
  7.2 0.0 all-gather.3.cloned.1.call-start
  7.2 0.7 all-gather.3.cloned.1.call-update
  7.9 0.0 reduce-scatter.3.cloned.1.call-start
  8.6 0.7 reduce.1
  9.3 0.7 fusion.22
  10.0 0.7 fusion.21
  10.7 26.6 %all-gather.3.cloned.1.call-done = bf16[32,8,1,4096]{3,0,2,1:T(8,128)(2,1)} async-done(((bf16[32,1,1,4096]{3,0,2,1:T(8,128)(2,1)}), bf16[32,8,1,4096]{3,0,2,1:T(8,128)(2,1)}) %all-gather.3.cloned.1.call-update) | async-done | bytes 2097168 | tf_op jit(solution)/shard_map/all_gather | solution.py:18
  37.3 2.7 copy.18
  40.1 2.4 reshape.89
  42.5 2.9 copy.19
  45.4 3.2 gather_fusion
  48.6 14.9 %broadcast_multiply_fusion.1 = f32[384,32,128]{2,1,0:T(8,128)} fusion(f32[384]{0:T(512)S(1)} %get-tuple-element.6, bf16[1,1,384,128,128]{4,3,2,1,0:T(8,128)(2,1)} %param.5, bf16[384,32,128]{2,1,0:T(8,128)(2,1)} %gather_fusion, pred[384]{0:T(512)(128)(4,1)S(1)} %get-tuple-element.7), kind=kOutput, calls=%fused_computation.15 | convolution fusion | flops 405798912 | bytes 22022016 | tf_op jit(solution)/shard_map/ksj,sij->ksi/dot_general | solution.py:29
  63.5 4.3 %broadcast_in_dim.28 = f32[32,512,128]{2,0,1:T(8,128)} broadcast(f32[]{:T(128)} %constant.18.clone.1), dimensions={} | broadcast | bytes 8388612 | tf_op jit(solution)/shard_map/broadcast_in_dim | solution.py:35
  67.8 51.2 %scatter_fusion = f32[32,512,128]{2,0,1:T(8,128)} fusion(f32[32,512,128]{2,0,1:T(8,128)} %broadcast_in_dim.28, s32[384]{0:T(512)S(1)} %fusion.21, f32[384,32,128]{2,1,0:T(8,128)} %broadcast_multiply_fusion.1), kind=kCustom, calls=%fused_computation.2 | custom fusion | flops 1572864 | bytes 18875904 | tf_op jit(solution)/shard_map/scatter-add | solution.py:30
  119.1 7.1 %copy_bitcast_fusion = f32[32,65536]{1,0:T(8,128)} fusion(f32[32,512,128]{2,0,1:T(8,128)} %scatter_fusion), kind=kLoop, calls=%fused_computation.8 | loop fusion | bytes 16777216 | tf_op jit(solution)/shard_map/reshape | solution.py:36
  126.2 0.0 copy-start
  126.2 0.0 reduce-scatter.3.cloned.1.call-update
  126.2 0.0 all-gather.5.cloned.1.call-start
  126.3 85.6 %reduce-scatter.3.cloned.1.call-done = f32[32,4096]{1,0:T(8,128)} async-done(((f32[32,65536]{1,0:T(8,128)}), f32[32,4096]{1,0:T(8,128)}) %reduce-scatter.3.cloned.1.call-update) | async-done | bytes 524304 | tf_op jit(solution)/shard_map/reduce_scatter | solution.py:37
  211.8 1.8 convert_element_type.14
  213.6 0.0 all-gather.5.cloned.1.call-update
  213.6 0.2 reduce-scatter.5.cloned.1.call-start
  213.9 0.0 copy-done
  213.9 51.6 %all-gather.5.cloned.1.call-done = bf16[32,65536]{1,0:T(8,128)(2,1)} async-done(((bf16[32,4096]{1,0:T(8,128)(2,1)}), bf16[32,65536]{1,0:T(8,128)(2,1)}) %all-gather.5.cloned.1.call-update) | async-done | bytes 4194320 | tf_op jit(solution)/shard_map/all_gather | solution.py:39
  265.6 4.9 %copy_bitcast_fusion.1 = bf16[32,512,128]{2,0,1:T(8,128)(2,1)} fusion(bf16[32,65536]{1,0:T(8,128)(2,1)} %all-gather.5.cloned.1.call-done), kind=kLoop, calls=%fused_computation.9 | loop fusion | bytes 8388608 | tf_op jit(solution)/shard_map/reshape | solution.py:40
  270.4 3.4 gather_fusion.1
  273.9 9.0 %broadcast_multiply_fusion = f32[384,32,128]{2,1,0:T(8,128)} fusion(f32[384]{0:T(512)S(1)} %get-tuple-element.6, bf16[1,1,384,128,128]{4,3,2,1,0:T(8,128)(2,1)} %param.5, bf16[384,32,128]{2,1,0:T(8,128)(2,1)S(1)} %gather_fusion.1, pred[384]{0:T(512)(128)(4,1)S(1)} %compare_and_fusion), kind=kOutput, calls=%fused_computation.14 | convolution fusion | flops 405798912 | bytes 22022016 | tf_op jit(solution)/shard_map/ksi,sij->ksj/dot_general | solution.py:45
  282.9 2.6 broadcast_in_dim.31
  285.5 51.3 %scatter_fusion.1 = f32[32,256,128]{2,0,1:T(8,128)} fusion(f32[32,256,128]{2,0,1:T(8,128)} %broadcast_in_dim.31, s32[384]{0:T(512)S(1)} %fusion.22, f32[384,32,128]{2,1,0:T(8,128)} %broadcast_multiply_fusion), kind=kCustom, calls=%fused_computation.3 | custom fusion | flops 1572864 | bytes 18875904 | tf_op jit(solution)/shard_map/scatter-add | solution.py:46
  336.8 6.5 %copy.22 = f32[32,256,128]{2,1,0:T(8,128)} copy(f32[32,256,128]{2,0,1:T(8,128)} %scatter_fusion.1) | data formatting | bytes 8388608 | tf_op jit(solution)/shard_map/scatter-add | solution.py:46
  343.3 5.0 %reshape.92 = f32[32,8,1,4096]{3,1,0,2:T(8,128)} reshape(f32[32,256,128]{2,1,0:T(8,128)} %copy.22) | data formatting | bytes 8388608 | tf_op jit(solution)/shard_map/reshape | solution.py:49
  348.3 6.5 %copy.23 = f32[32,8,1,4096]{3,0,2,1:T(8,128)} copy(f32[32,8,1,4096]{3,1,0,2:T(8,128)} %reshape.92) | data formatting | bytes 8388608 | tf_op jit(solution)/shard_map/reshape | solution.py:49
  354.8 0.0 reduce-scatter.5.cloned.1.call-update
  354.9 37.6 %reduce-scatter.5.cloned.1.call-done = f32[32,1,1,4096]{3,0,2,1:T(8,128)} async-done(((f32[32,8,1,4096]{3,0,2,1:T(8,128)}), f32[32,1,1,4096]{3,0,2,1:T(8,128)}) %reduce-scatter.5.cloned.1.call-update) | async-done | bytes 524304 | tf_op jit(solution)/shard_map/reduce_scatter | solution.py:50
  392.5 1.8 convert_element_type.15
  (5 shorter events, 0.0 us)
Async XLA Ops:
  7.2 30.2 %all-gather.3.cloned.1.call-start = ((), (), s32[]{:S(2)}) async-start(), calls=%async_computation.2 | async-start | bytes 2359296 | tf_op jit(solution)/shard_map/all_gather | solution.py:18
  7.9 203.9 %reduce-scatter.3.cloned.1.call-start = ((), (), s32[]{:S(2)}) async-start(), calls=%async_computation.3 | async-start | bytes 8912896 | tf_op jit(solution)/shard_map/reduce_scatter | solution.py:37
  126.2 87.7 %copy-start = (s32[1,1,384]{2,1,0:T(1,128)S(1)}, s32[1,1,384]{2,1,0:T(1,128)}, u32[]{:S(2)}) copy-start(s32[1,1,384]{2,1,0:T(1,128)} %param.6) | copy-start | bytes 4612
  126.2 139.3 %all-gather.5.cloned.1.call-start = ((), (), s32[]{:S(2)}) async-start(), calls=%async_computation.4 | async-start | bytes 4456448 | tf_op jit(solution)/shard_map/all_gather | solution.py:39
  213.6 178.8 %reduce-scatter.5.cloned.1.call-start = ((), (), s32[]{:S(2)}) async-start(), calls=%async_computation.5 | async-start | bytes 4718592 | tf_op jit(solution)/shard_map/reduce_scatter | solution.py:50
Sparse Core Ops, SparseCore 0:
  9.7 27.5 all-gather.2
  126.3 85.4 reduce-scatter.2
  214.6 50.9 all-gather.4
  355.0 37.4 reduce-scatter.4
where the time goes:
time: 402 us; the launch traced here: 401 us
  waiting for transfers between devices  202 us (50%)
  other arithmetic  108 us (27%)
  local copies, waits for them, and re-layouts  51.6 us (13%)
  matrix products  24 us (6%)
  between operations  14.4 us (4%)
    reduce_scatter x1, waiting for transfers between devices, per_device(): lax.psum_scatter(partial_rows, 'col', scatter_dimension=1, tiled=True)  85.6 us
    all_gather x1, waiting for transfers between devices, per_device(): row_image = lax.all_gather(image, 'col', axis=1, tiled=True)  51.6 us
    scatter-add x1, other arithmetic, backward_terms(): return totals.at[:, col_index].add(product * slot_mask[None, :, None])  51.3 us
    scatter-add x1, other arithmetic, forward_terms(): return totals.at[:, row_index].add(product * slot_mask[None, :, None])  51.2 us
    reduce_scatter x1, waiting for transfers between devices, per_device(): lax.psum_scatter(partial_cols, 'row', scatter_dimension=1, tiled=True)  37.6 us
    all_gather x1, waiting for transfers between devices, per_device(): gathered = lax.all_gather(vectors, 'row', axis=1, tiled=True)  26.6 us
    dot_general x1, matrix products, forward_terms(): jnp.einsum('ksj,sij->ksi', picked, tile_block, preferred_element_type=jnp...  14.9 us
    reshape x2, local copies, waits for them, and re-layouts, per_device(): backward_sum.reshape(vec_cols, row_devices, 1, vectors.shape[3])  11.5 us
  transfers between devices with their start and end apart: 4, of which 4 were waited for; matrix products, arithmetic and copies ran while one was open for 1% of the time, Pallas kernels for 0%

commit v1 on v0

--- a/solution.py
+++ b/solution.py
@@ -15,7 +15,21 @@
     live_mask = (jnp.arange(slot_count, dtype=jnp.int32) < live_count).astype(jnp.float32)
     row_devices = lax.axis_size("row")
     col_devices = lax.axis_size("col")
-    gathered = lax.all_gather(vectors, "row", axis=1, tiled=True)
+    ways, here, step = (lax.axis_size("row"), lax.axis_index("row"), vectors.shape[1])
+    shape = [n * ways if d == 1 else n for d, n in enumerate(vectors.shape)]
+    full = lax.dynamic_update_slice_in_dim(
+        jnp.zeros(shape, vectors.dtype), vectors, here * step, axis=1
+    )
+    going_up = going_down = vectors
+    for far in range(1, ways // 2 + 1):
+        going_up = lax.ppermute(going_up, "row", [(d, (d + 1) % ways) for d in range(ways)])
+        full = lax.dynamic_update_slice_in_dim(full, going_up, (here - far) % ways * step, axis=1)
+        if 2 * far < ways:
+            going_down = lax.ppermute(going_down, "row", [(d, (d - 1) % ways) for d in range(ways)])
+            full = lax.dynamic_update_slice_in_dim(
+                full, going_down, (here + far) % ways * step, axis=1
+            )
+    gathered = full
     blk_cols = gathered.shape[1] * gathered.shape[3] // tile_size
     blk_rows = blk_cols * col_devices // row_devices
     col_vectors = gathered.reshape(vec_cols, blk_cols, tile_size)

time: 402 us -> 444 us (1.10)
  local copies, waits for them, and re-layouts: 51.6 us -> 98.5 us
  waiting for transfers between devices: 202 us -> 188 us
  starting transfers between devices: 0.34 us -> 8.98 us
    dynamic_update_slice x0 -> x8, local copies, waits for them, and re-layouts: none -> 40.3 us  [the longest x4 20.1 us: per_device(): lax.dynamic_update_slice_in_dim(full, going_up, (here - far) % ways * ste...]
    all_gather x1 -> x0, waiting for transfers between devices: 26.6 us -> none  [per_device(): gathered = lax.all_gather(vectors, 'row', axis=1, tiled=True)]
    ppermute x0 -> x7, waiting for transfers between devices: none -> 11 us  [the longest x4 10.9 us: per_device(): lax.ppermute(going_up, 'row', [(d, (d + 1) % ways) for d in range(ways)])]
    ppermute x0 -> x7, starting transfers between devices: none -> 8.86 us  [the longest x3 8.83 us: per_device(): lax.ppermute(going_down, 'row', [(d, (d - 1) % ways) for d in range(ways)])]
    ppermute x0 -> x7, local copies, waits for them, and re-layouts: none -> 7.64 us  [the longest x4 5.05 us: per_device(): lax.ppermute(going_up, 'row', [(d, (d + 1) % ways) for d in range(ways)])]
  transfers between devices with their start and end apart: 4 -> 10, of which waited for: 4 -> 6; matrix products, arithmetic and copies ran while one was open for 1% -> 10% of each run, Pallas kernels for 0% -> 0%
where the time goes in v1:
time: 444 us; the launch traced here: 443 us
  waiting for transfers between devices  188 us (42%)
  other arithmetic  108 us (24%)
  local copies, waits for them, and re-layouts  98.5 us (22%)
  matrix products  24 us (5%)
  between operations  14.8 us (3%)
  starting transfers between devices  8.98 us (2%)
    reduce_scatter x1, waiting for transfers between devices, per_device(): lax.psum_scatter(partial_rows, 'col', scatter_dimension=1, tiled=True)  87.7 us
    all_gather x1, waiting for transfers between devices, per_device(): row_image = lax.all_gather(image, 'col', axis=1, tiled=True)  51.8 us
    scatter-add x1, other arithmetic, backward_terms(): return totals.at[:, col_index].add(product * slot_mask[None, :, None])  51.3 us
    scatter-add x1, other arithmetic, forward_terms(): return totals.at[:, row_index].add(product * slot_mask[None, :, None])  51.2 us
    reduce_scatter x1, waiting for transfers between devices, per_device(): lax.psum_scatter(partial_cols, 'row', scatter_dimension=1, tiled=True)  37.6 us
    dynamic_update_slice x4, local copies, waits for them, and re-layouts, per_device(): lax.dynamic_update_slice_in_dim(full, going_up, (here - far) % ways * ste...  20.1 us
    dynamic_update_slice x3, local copies, waits for them, and re-layouts, per_device(): lax.dynamic_update_slice_in_dim(full, going_down, (here + far) % ways * s...  15.1 us
    dot_general x1, matrix products, forward_terms(): jnp.einsum('ksj,sij->ksi', picked, tile_block, preferred_element_type=jnp...  14.9 us
  transfers between devices with their start and end apart: 10, of which 6 were waited for; matrix products, arithmetic and copies ran while one was open for 10% of the time, Pallas kernels for 0%

profile of v1, /device:TPU:0, one launch (start us, length us, event | category | flops | bytes accessed | tf_op | source)
XLA Modules:
  0.0 442.6 jit_solution(10380057657508186000)
XLA Ops:
  7.2 2.9 collective-permute-start.1
  10.2 4.3 collective-permute-done
  14.4 3.0 collective-permute-start.3
  17.4 4.0 collective-permute-done.2
  21.5 0.7 fusion.22
  22.2 0.7 fusion.21
  22.9 2.9 collective-permute-start.5
  25.8 2.6 collective-permute-done.4
  28.5 1.5 copy.32
  30.1 0.7 reduce.1
  31.5 0.2 broadcast_in_dim.33
  31.7 5.0 %dynamic_update_slice.24 = bf16[32,8,1,4096]{3,1,0,2:T(8,128)(2,1)S(1)} dynamic-update-slice(bf16[32,8,1,4096]{3,1,0,2:T(8,128)(2,1)S(1)} %broadcast_in_dim.33, bf16[32,1,1,4096]{3,1,0,2:T(2,128)(2,1)S(1)} %copy.32, s32[]{:T(128)} %constant.78.clone.1, s32[]{:T(128)S(6)} %select_n.98, s32[]{:T(128)} %constant.78.clone.1, s32[]{:T(128)} %constant.78.clone.1) | dynamic-update-slice | bytes 524292 | tf_op jit(solution)/shard_map/dynamic_update_slice | solution.py:20
  36.8 1.5 copy.33
  38.3 5.0 %dynamic_update_slice.25 = bf16[32,8,1,4096]{3,1,0,2:T(8,128)(2,1)S(1)} dynamic-update-slice(bf16[32,8,1,4096]{3,1,0,2:T(8,128)(2,1)S(1)} %dynamic_update_slice.24, bf16[32,1,1,4096]{3,1,0,2:T(2,128)(2,1)S(1)} %copy.33, s32[]{:T(128)} %constant.78.clone.1, s32[]{:T(128)S(6)} %select_n.100, s32[]{:T(128)} %constant.78.clone.1, s32[]{:T(128)} %constant.78.clone.1) | dynamic-update-slice | bytes 524292 | tf_op jit(solution)/shard_map/dynamic_update_slice | solution.py:26
  43.3 0.5 copy.34
  43.9 5.0 %dynamic_update_slice.26 = bf16[32,8,1,4096]{3,1,0,2:T(8,128)(2,1)S(1)} dynamic-update-slice(bf16[32,8,1,4096]{3,1,0,2:T(8,128)(2,1)S(1)} %dynamic_update_slice.25, bf16[32,1,1,4096]{3,1,0,2:T(2,128)(2,1)S(1)} %copy.34, s32[]{:T(128)} %constant.78.clone.1, s32[]{:T(128)S(6)} %select_n.102, s32[]{:T(128)} %constant.78.clone.1, s32[]{:T(128)} %constant.78.clone.1) | dynamic-update-slice | bytes 524292 | tf_op jit(solution)/shard_map/dynamic_update_slice | solution.py:29
  49.0 1.5 copy.35
  50.5 5.0 %dynamic_update_slice.27 = bf16[32,8,1,4096]{3,1,0,2:T(8,128)(2,1)S(1)} dynamic-update-slice(bf16[32,8,1,4096]{3,1,0,2:T(8,128)(2,1)S(1)} %dynamic_update_slice.26, bf16[32,1,1,4096]{3,1,0,2:T(2,128)(2,1)S(1)} %copy.35, s32[]{:T(128)} %constant.78.clone.1, s32[]{:T(128)S(6)} %select_n.104, s32[]{:T(128)} %constant.78.clone.1, s32[]{:T(128)} %constant.78.clone.1) | dynamic-update-slice | bytes 524292 | tf_op jit(solution)/shard_map/dynamic_update_slice | solution.py:26
  55.5 0.5 copy.36
  56.1 5.0 %dynamic_update_slice.28 = bf16[32,8,1,4096]{3,1,0,2:T(8,128)(2,1)S(1)} dynamic-update-slice(bf16[32,8,1,4096]{3,1,0,2:T(8,128)(2,1)S(1)} %dynamic_update_slice.27, bf16[32,1,1,4096]{3,1,0,2:T(2,128)(2,1)S(1)} %copy.36, s32[]{:T(128)} %constant.78.clone.1, s32[]{:T(128)S(6)} %select_n.106, s32[]{:T(128)} %constant.78.clone.1, s32[]{:T(128)} %constant.78.clone.1) | dynamic-update-slice | bytes 524292 | tf_op jit(solution)/shard_map/dynamic_update_slice | solution.py:29
  61.1 0.5 copy.37
  61.7 5.0 %dynamic_update_slice.29 = bf16[32,8,1,4096]{3,1,0,2:T(8,128)(2,1)S(1)} dynamic-update-slice(bf16[32,8,1,4096]{3,1,0,2:T(8,128)(2,1)S(1)} %dynamic_update_slice.28, bf16[32,1,1,4096]{3,1,0,2:T(2,128)(2,1)S(1)} %copy.37, s32[]{:T(128)} %constant.78.clone.1, s32[]{:T(128)S(6)} %select_n.108, s32[]{:T(128)} %constant.78.clone.1, s32[]{:T(128)} %constant.78.clone.1) | dynamic-update-slice | bytes 524292 | tf_op jit(solution)/shard_map/dynamic_update_slice | solution.py:26
  66.7 1.5 copy.38
  68.2 5.0 %dynamic_update_slice.30 = bf16[32,8,1,4096]{3,1,0,2:T(8,128)(2,1)S(1)} dynamic-update-slice(bf16[32,8,1,4096]{3,1,0,2:T(8,128)(2,1)S(1)} %dynamic_update_slice.29, bf16[32,1,1,4096]{3,1,0,2:T(2,128)(2,1)S(1)} %copy.38, s32[]{:T(128)} %constant.78.clone.1, s32[]{:T(128)S(6)} %select_n.110, s32[]{:T(128)} %constant.78.clone.1, s32[]{:T(128)} %constant.78.clone.1) | dynamic-update-slice | bytes 524292 | tf_op jit(solution)/shard_map/dynamic_update_slice | solution.py:29
  73.3 1.5 copy.39
  74.8 5.0 %dynamic_update_slice.31 = bf16[32,8,1,4096]{3,1,0,2:T(8,128)(2,1)S(1)} dynamic-update-slice(bf16[32,8,1,4096]{3,1,0,2:T(8,128)(2,1)S(1)} %dynamic_update_slice.30, bf16[32,1,1,4096]{3,1,0,2:T(2,128)(2,1)S(1)} %copy.39, s32[]{:T(128)} %constant.78.clone.1, s32[]{:T(128)S(6)} %select_n.112, s32[]{:T(128)} %constant.78.clone.1, s32[]{:T(128)} %constant.78.clone.1) | dynamic-update-slice | bytes 524292 | tf_op jit(solution)/shard_map/dynamic_update_slice | solution.py:26
  79.8 2.4 reshape.89
  82.2 2.9 copy.40
  85.1 3.2 gather_fusion
  88.3 14.9 %broadcast_multiply_fusion.1 = f32[384,32,128]{2,1,0:T(8,128)} fusion(f32[384]{0:T(512)S(1)} %get-tuple-element.6, bf16[1,1,384,128,128]{4,3,2,1,0:T(8,128)(2,1)} %param.5, bf16[384,32,128]{2,1,0:T(8,128)(2,1)} %gather_fusion, pred[384]{0:T(512)(128)(4,1)S(1)} %get-tuple-element.7), kind=kOutput, calls=%fused_computation.15 | convolution fusion | flops 405798912 | bytes 22022016 | tf_op jit(solution)/shard_map/ksj,sij->ksi/dot_general | solution.py:43
  103.3 4.3 broadcast_in_dim.31
  107.6 51.2 %scatter_fusion = f32[32,512,128]{2,0,1:T(8,128)} fusion(f32[32,512,128]{2,0,1:T(8,128)} %broadcast_in_dim.31, s32[384]{0:T(512)S(1)} %fusion.21, f32[384,32,128]{2,1,0:T(8,128)} %broadcast_multiply_fusion.1), kind=kCustom, calls=%fused_computation.2 | custom fusion | flops 1572864 | bytes 18875904 | tf_op jit(solution)/shard_map/scatter-add | solution.py:44
  158.8 7.1 %copy_bitcast_fusion = f32[32,65536]{1,0:T(8,128)} fusion(f32[32,512,128]{2,0,1:T(8,128)} %scatter_fusion), kind=kLoop, calls=%fused_computation.8 | loop fusion | bytes 16777216 | tf_op jit(solution)/shard_map/reshape | solution.py:50
  166.0 0.0 all-gather.2.cloned.1.call-start
  166.0 87.7 %reduce-scatter.3.cloned.1.call-done = f32[32,4096]{1,0:T(8,128)} async-done(((f32[32,65536]{1,0:T(8,128)}), f32[32,4096]{1,0:T(8,128)}) %reduce-scatter.3.cloned.1.call-update) | async-done | bytes 524304 | tf_op jit(solution)/shard_map/reduce_scatter | solution.py:51
  253.7 1.8 convert_element_type.14
  255.5 0.0 reduce-scatter.5.cloned.1.call-start
  255.6 51.8 %all-gather.2.cloned.1.call-done = bf16[32,65536]{1,0:T(8,128)(2,1)} async-done(((bf16[32,4096]{1,0:T(8,128)(2,1)}), bf16[32,65536]{1,0:T(8,128)(2,1)}) %all-gather.2.cloned.1.call-update) | async-done | bytes 4194320 | tf_op jit(solution)/shard_map/all_gather | solution.py:53
  307.4 4.9 %copy_bitcast_fusion.1 = bf16[32,512,128]{2,0,1:T(8,128)(2,1)} fusion(bf16[32,65536]{1,0:T(8,128)(2,1)} %all-gather.2.cloned.1.call-done), kind=kLoop, calls=%fused_computation.9 | loop fusion | bytes 8388608 | tf_op jit(solution)/shard_map/reshape | solution.py:54
  312.3 3.4 gather_fusion.1
  315.7 9.0 %broadcast_multiply_fusion = f32[384,32,128]{2,1,0:T(8,128)} fusion(f32[384]{0:T(512)S(1)} %get-tuple-element.6, bf16[1,1,384,128,128]{4,3,2,1,0:T(8,128)(2,1)} %param.5, bf16[384,32,128]{2,1,0:T(8,128)(2,1)S(1)} %gather_fusion.1, pred[384]{0:T(512)(128)(4,1)S(1)} %compare_and_fusion), kind=kOutput, calls=%fused_computation.14 | convolution fusion | flops 405798912 | bytes 22022016 | tf_op jit(solution)/shard_map/ksi,sij->ksj/dot_general | solution.py:59
  324.7 2.6 broadcast_in_dim.35
  327.3 51.3 %scatter_fusion.1 = f32[32,256,128]{2,0,1:T(8,128)} fusion(f32[32,256,128]{2,0,1:T(8,128)} %broadcast_in_dim.35, s32[384]{0:T(512)S(1)} %fusion.22, f32[384,32,128]{2,1,0:T(8,128)} %broadcast_multiply_fusion), kind=kCustom, calls=%fused_computation.3 | custom fusion | flops 1572864 | bytes 18875904 | tf_op jit(solution)/shard_map/scatter-add | solution.py:60
  378.6 6.5 %copy.43 = f32[32,256,128]{2,1,0:T(8,128)} copy(f32[32,256,128]{2,0,1:T(8,128)} %scatter_fusion.1) | data formatting | bytes 8388608 | tf_op jit(solution)/shard_map/scatter-add | solution.py:60
  385.2 5.0 %reshape.92 = f32[32,8,1,4096]{3,1,0,2:T(8,128)} reshape(f32[32,256,128]{2,1,0:T(8,128)} %copy.43) | data formatting | bytes 8388608 | tf_op jit(solution)/shard_map/reshape | solution.py:63
  390.1 6.5 %copy.44 = f32[32,8,1,4096]{3,0,2,1:T(8,128)} copy(f32[32,8,1,4096]{3,1,0,2:T(8,128)} %reshape.92) | data formatting | bytes 8388608 | tf_op jit(solution)/shard_map/reshape | solution.py:63
  396.7 37.6 %reduce-scatter.5.cloned.1.call-done = f32[32,1,1,4096]{3,0,2,1:T(8,128)} async-done(((f32[32,8,1,4096]{3,0,2,1:T(8,128)}), f32[32,1,1,4096]{3,0,2,1:T(8,128)}) %reduce-scatter.5.cloned.1.call-update) | async-done | bytes 524304 | tf_op jit(solution)/shard_map/reduce_scatter | solution.py:64
  434.3 1.8 convert_element_type.15
  (23 shorter events, 0.2 us)
Async XLA Ops:
  7.2 246.5 %reduce-scatter.3.cloned.1.call-start = ((), (), s32[]{:S(2)}) async-start(), calls=%async_computation.2 | async-start | bytes 8912896 | tf_op jit(solution)/shard_map/reduce_scatter | solution.py:51
  7.2 7.2 %collective-permute-start = (bf16[32,1,1,4096]{3,0,2,1:T(8,128)(2,1)}, bf16[32,1,1,4096]{3,0,2,1:T(8,128)(2,1)S(1)}, u32[]{:S(2)}, u32[]{:S(2)}) collective-permute-start(bf16[32,1,1,4096]{3,0,2,1:T(8,128)(2,1)} %param.9), channel_id=1, source_target_pairs={{0,16},{16,32},{32,48},{48,64},{64,80},{80,96},{96,112},{112,0},{1... | collective-permute-start | bytes 786440 | tf_op jit(solution)/shard_map/ppermute | solution.py:25
  7.2 7.2 %collective-permute-start.1 = (bf16[32,1,1,4096]{3,0,2,1:T(8,128)(2,1)}, bf16[32,1,1,4096]{3,0,2,1:T(8,128)(2,1)S(1)}, u32[]{:S(2)}, u32[]{:S(2)}) collective-permute-start(bf16[32,1,1,4096]{3,0,2,1:T(8,128)(2,1)} %param.9), channel_id=1, source_target_pairs={{0,112},{16,0},{32,16},{48,32},{64,48},{80,64},{96,80},{112,96},{1... | collective-permute-start | bytes 786440 | tf_op jit(solution)/shard_map/ppermute | solution.py:28
  14.4 7.0 %copy-start.1 = (bf16[32,1,1,4096]{3,0,2,1:T(8,128)(2,1)}, bf16[32,1,1,4096]{3,0,2,1:T(8,128)(2,1)S(1)}, u32[]{:S(2)}) copy-start(bf16[32,1,1,4096]{3,0,2,1:T(8,128)(2,1)S(1)} %collective-permute-done) | copy-start | bytes 786436
  14.4 7.0 %collective-permute-start.2 = (bf16[32,1,1,4096]{3,0,2,1:T(8,128)(2,1)S(1)}, bf16[32,1,1,4096]{3,0,2,1:T(8,128)(2,1)S(1)}, u32[]{:S(2)}, u32[]{:S(2)}) collective-permute-start(bf16[32,1,1,4096]{3,0,2,1:T(8,128)(2,1)S(1)} %collective-permute-done), channel_id=1, source_target_pairs={{0,16},{16,32},{32,48},{48,64},{64,80},{80,96},{96,112},{112,0},{1... | collective-permute-start | bytes 786440 | tf_op jit(solution)/shard_map/ppermute | solution.py:25
  14.4 8.4 %collective-permute-start.3 = (bf16[32,1,1,4096]{3,0,2,1:T(8,128)(2,1)S(1)}, bf16[32,1,1,4096]{3,0,2,1:T(8,128)(2,1)S(1)}, u32[]{:S(2)}, u32[]{:S(2)}) collective-permute-start(bf16[32,1,1,4096]{3,0,2,1:T(8,128)(2,1)S(1)} %collective-permute-done.1), channel_id=1, source_target_pairs={{0,112},{16,0},{32,16},{48,32},{64,48},{80,64},{96,80},{112,96},{1... | collective-permute-start | bytes 786440 | tf_op jit(solution)/shard_map/ppermute | solution.py:28
  21.5 7.0 %copy-start = (bf16[32,1,1,4096]{3,0,2,1:T(8,128)(2,1)}, bf16[32,1,1,4096]{3,0,2,1:T(8,128)(2,1)S(1)}, u32[]{:S(2)}) copy-start(bf16[32,1,1,4096]{3,0,2,1:T(8,128)(2,1)S(1)} %collective-permute-done.2) | copy-start | bytes 786436
  21.5 7.0 %collective-permute-start.4 = (bf16[32,1,1,4096]{3,0,2,1:T(8,128)(2,1)S(1)}, bf16[32,1,1,4096]{3,0,2,1:T(8,128)(2,1)S(1)}, u32[]{:S(2)}, u32[]{:S(2)}) collective-permute-start(bf16[32,1,1,4096]{3,0,2,1:T(8,128)(2,1)S(1)} %collective-permute-done.2), channel_id=1, source_target_pairs={{0,16},{16,32},{32,48},{48,64},{64,80},{80,96},{96,112},{112,0},{1... | collective-permute-start | bytes 786440 | tf_op jit(solution)/shard_map/ppermute | solution.py:25
  22.9 43.8 %collective-permute-start.5 = (bf16[32,1,1,4096]{3,0,2,1:T(8,128)(2,1)S(1)}, bf16[32,1,1,4096]{3,0,2,1:T(8,128)(2,1)}, u32[]{:S(2)}, u32[]{:S(2)}) collective-permute-start(bf16[32,1,1,4096]{3,0,2,1:T(8,128)(2,1)S(1)} %collective-permute-done.3), channel_id=1, source_target_pairs={{0,112},{16,0},{32,16},{48,32},{64,48},{80,64},{96,80},{112,96},{1... | collective-permute-start | bytes 786440 | tf_op jit(solution)/shard_map/ppermute | solution.py:28
  28.5 44.8 %collective-permute-start.6 = (bf16[32,1,1,4096]{3,0,2,1:T(8,128)(2,1)S(1)}, bf16[32,1,1,4096]{3,0,2,1:T(8,128)(2,1)}, u32[]{:S(2)}, u32[]{:S(2)}) collective-permute-start(bf16[32,1,1,4096]{3,0,2,1:T(8,128)(2,1)S(1)} %collective-permute-done.4), channel_id=1, source_target_pairs={{0,16},{16,32},{32,48},{48,64},{64,80},{80,96},{96,112},{112,0},{1... | collective-permute-start | bytes 786440 | tf_op jit(solution)/shard_map/ppermute | solution.py:25
  165.9 89.6 %copy-start.2 = (s32[1,1,384]{2,1,0:T(1,128)S(1)}, s32[1,1,384]{2,1,0:T(1,128)}, u32[]{:S(2)}) copy-start(s32[1,1,384]{2,1,0:T(1,128)} %param.6) | copy-start | bytes 4612
  166.0 141.4 %all-gather.2.cloned.1.call-start = ((), (), s32[]{:S(2)}) async-start(), calls=%async_computation.3 | async-start | bytes 4456448 | tf_op jit(solution)/shard_map/all_gather | solution.py:53
  255.5 178.8 %reduce-scatter.5.cloned.1.call-start = ((), (), s32[]{:S(2)}) async-start(), calls=%async_computation.4 | async-start | bytes 4718592 | tf_op jit(solution)/shard_map/reduce_scatter | solution.py:64
Sparse Core Ops, SparseCore 0:
  166.1 87.5 reduce-scatter.2
  256.4 50.9 all-gather.1
  396.8 37.4 reduce-scatter.4
